TPU v7x, 256 devices: a whole 4x4x8 slice. The times are simulated.
256 devices in a mesh: tx: 4 (over y), ty: 2 (over z_lo), ea: 32 (over z_hi, x, core).
Axes of the slice: x: 4, y: 4, z: 8 (z_hi: 4, z_lo: 2; z = z_hi * 2 + z_lo), core: 2. Of those that a mesh axis runs over, the one named last changes fastest.
Arguments:
- science: float32 [32, 512, 512], P('ea', 'tx', 'ty'), may hold values from -6 to 6
- inv_variance: float32 [32, 512, 512], P('ea', 'tx', 'ty'), may hold values from 0.25 to 4
- psf_taps: float32 [32, 9], P('ea'), may hold values from 0.05 to 1
- epoch_times: int32 [32], replicated, may hold values from 0 to 256, as said below
- velocities: int32 [192, 2], P('ea'), may hold values from -15 to 15
Outputs:
- likelihood: float32 [192, 512, 512], P('ea', 'tx', 'ty')
Inputs may be any that keep to these rules, and one draw needn't show every extreme that they name: `epoch_times`: the first epoch has time 0 and the last has time 256.
All inputs are finite; a program needn't handle non-finite values.
Results may differ from a plain program's by a relative error of at most 0.0053.
Values may be sent and summed in bfloat16 or wider, within the bound.
A program may use at most 64 MiB of HBM per device.

v0:
```python
import jax
import jax.numpy as jnp
from jax import lax
from jax.sharding import PartitionSpec as P

REACH = 32
PR = 4


def extended(cells, sides, width):
    for axis, dim in sides:
        count = lax.axis_size(axis)
        ends = count - 1
        head = lax.slice_in_dim(cells, 0, width, axis=dim)
        tail = lax.slice_in_dim(cells, cells.shape[dim] - width, cells.shape[dim], axis=dim)
        cells = jnp.concatenate(
            [
                lax.ppermute(tail, axis, [(i, (i + 1) % count) for i in range(ends)]),
                cells,
                lax.ppermute(head, axis, [((i + 1) % count, i) for i in range(ends)]),
            ],
            axis=dim,
        )
    return cells


def blur(field, kern):
    count = kern.shape[1]
    rows = field.shape[1] - count + 1
    acc = kern[:, 0, None, None] * field[:, 0:rows, :]
    for k in range(1, count):
        acc = acc + kern[:, k, None, None] * field[:, k : k + rows, :]
    cols = acc.shape[2] - count + 1
    out = kern[:, 0, None, None] * acc[:, :, 0:cols]
    for k in range(1, count):
        out = out + kern[:, k, None, None] * acc[:, :, k : k + cols]
    return out


def spline_taps(speed, tvals):
    moved = jnp.floor_divide(speed * tvals, 8)
    whole = jnp.floor_divide(moved, 16)
    frac = (moved - 16 * whole).astype(jnp.float32) / 16.0
    frac2 = frac * frac
    frac3 = frac2 * frac
    weights = jnp.stack(
        [
            (1.0 - frac) ** 3 / 6.0,
            (3.0 * frac3 - 6.0 * frac2 + 4.0) / 6.0,
            (-3.0 * frac3 + 3.0 * frac2 + 3.0 * frac + 1.0) / 6.0,
            frac3 / 6.0,
        ],
        -1,
    )
    return (whole, weights.astype(jnp.bfloat16))


def band_matrix(whole, weights, count, span):
    target = lax.broadcasted_iota(jnp.int32, (1, count, span), 2)
    source = lax.broadcasted_iota(jnp.int32, (1, count, span), 1)
    offset = target - source - (REACH + whole - 1)[:, None, None]
    matrix = jnp.zeros((whole.shape[0], count, span), jnp.bfloat16)
    for a in range(4):
        matrix = matrix + jnp.where(
            offset == a, weights[:, a, None, None], jnp.zeros((), jnp.bfloat16)
        )
    return matrix


def stack_block(padded, tvals, velocities, out_rows, out_cols):
    pad_rows = padded.shape[2]
    pad_cols = padded.shape[3]

    def one_hyp(speed):
        whole_r, w_r = spline_taps(speed[0], tvals)
        whole_c, w_c = spline_taps(speed[1], tvals)
        row_band = band_matrix(whole_r, w_r, out_rows, pad_rows)
        col_band = band_matrix(whole_c, w_c, out_cols, pad_cols)
        moved_rows = jnp.einsum(
            "erp,eipk->eirk", row_band, padded, preferred_element_type=jnp.float32
        ).astype(jnp.bfloat16)
        return jnp.einsum("eirk,eck->irc", moved_rows, col_band, preferred_element_type=jnp.float32)

    return lax.map(one_hyp, velocities)


def shards(science, inv_variance, psf_taps, epoch_times, velocities):
    out_rows = science.shape[1]
    out_cols = science.shape[2]
    kern_p = psf_taps / jnp.sum(psf_taps, axis=1, keepdims=True)
    kern_q = kern_p * kern_p
    raw_pair = jnp.stack([science * inv_variance, inv_variance], 0)
    framed = extended(raw_pair, (("tx", 2), ("ty", 3)), PR)
    psi = blur(framed[0], kern_p).astype(jnp.bfloat16)
    phi = blur(framed[1], kern_q).astype(jnp.bfloat16)
    images = jnp.stack([psi, phi], 1)
    every_epoch = lax.all_gather(images, "ea", axis=0, tiled=True)
    padded = extended(every_epoch, (("tx", 2), ("ty", 3)), REACH)
    stacks = stack_block(padded, epoch_times, velocities, out_rows, out_cols)
    return stacks[:, 0] / jnp.sqrt(stacks[:, 1])


def solution(mesh):
    in_specs = (P("ea", "tx", "ty"), P("ea", "tx", "ty"), P("ea", None), P(), P("ea", None))
    out_specs = P("ea", "tx", "ty")
    return jax.shard_map(shards, mesh=mesh, in_specs=in_specs, out_specs=out_specs, check_vma=False)
```

profile of v0, /device:TPU:1, one launch (start us, length us, event | category | flops | bytes accessed | tf_op | source)
XLA Modules:
  0.0 319.9 jit_solution(10306133424879456887)
XLA Ops:
  8.2 4.0 %collective-permute-start = (f32[2,1,4,256]{3,2,1,0:T(4,128)S(1)}, f32[2,1,4,256]{3,2,1,0:T(4,128)S(1)}, u32[]{:S(2)}, u32[]{:S(2)}) collective-permute-start(f32[2,1,4,256]{3,2,1,0:T(4,128)S(1)} %get-tuple-element.184), channel_id=1, source_target_pairs={{0,64},{64,128},{128,192},{1,65},{65,129},{129,193},{2,66},{66,130... | collective-permute-start | bytes 24584 | tf_op jit(solution)/shard_map/ppermute | solution.py:18
  12.3 1.3 collective-permute-start.1
  14.8 1.3 fusion.139
  17.7 3.5 %collective-permute-start.2 = (f32[2,1,136,4]{3,2,1,0:T(8,128)S(1)}, f32[2,1,136,4]{3,2,1,0:T(8,128)S(1)}, u32[]{:S(2)}, u32[]{:S(2)}) collective-permute-start(f32[2,1,136,4]{3,2,1,0:T(8,128)S(1)} %get-tuple-element.182), channel_id=1, source_target_pairs={{0,32},{1,33},{2,34},{3,35},{4,36},{5,37},{6,38},{7,39},{8,40},{9,... | collective-permute-start | bytes 13064 | tf_op jit(solution)/shard_map/ppermute | solution.py:18
  21.3 1.3 collective-permute-start.3
  23.3 3.8 %collective-permute-done.3 = f32[2,1,136,4]{3,2,1,0:T(8,128)S(1)} collective-permute-done((f32[2,1,136,4]{3,2,1,0:T(8,128)S(1)}, f32[2,1,136,4]{3,2,1,0:T(8,128)S(1)}, u32[]{:S(2)}, u32[]{:S(2)}) %collective-permute-start.3) | collective-permute-done | bytes 4384 | tf_op jit(solution)/shard_map/ppermute | solution.py:20
  28.2 6.0 %fusion.111 = f32[1,128,264]{2,1,0:T(8,128)S(1)} fusion(f32[1,136,264]{2,1,0:T(8,128)S(1)} %get-tuple-element.180, f32[]{:T(128)} %bitcast.29, f32[]{:T(128)} %bitcast.28, f32[]{:T(128)} %bitcast.27, f32[]{:T(128)} %bitcast.26, f32[]{:T(128)} %bitcast.25, f32[]{:T(128)} %bitcast.24, f32[]{:T(128)} %bitcast.23, f32[]{:T(128)} %bitcast.22, f32[]{:T(128)} %bitcast.18), kind=kLoop, calls=%fused_computation.141 | loop fusion | flops 574464 | bytes 1351716 | tf_op jit(solution)/shard_map/add | solution.py:32
  34.3 6.2 %fusion.137 = bf16[1,1,128,256]{3,2,1,0:T(8,128)(2,1)S(1)} fusion(f32[1,128,264]{2,1,0:T(8,128)S(1)} %fusion.111, f32[]{:T(128)} %bitcast.29, f32[]{:T(128)} %bitcast.28, f32[]{:T(128)} %bitcast.27, f32[]{:T(128)} %bitcast.26, f32[]{:T(128)} %bitcast.25, f32[]{:T(128)} %bitcast.24, f32[]{:T(128)} %bitcast.23, f32[]{:T(128)} %bitcast.22, f32[]{:T(128)} %bitcast.18), kind=kLoop, calls=%fused_computation.195 | loop fusion | flops 589824 | bytes 1245220 | tf_op jit(solution)/shard_map/stack | solution.py:96
  40.4 5.7 %fusion.103 = f32[1,128,264]{2,1,0:T(8,128)S(1)} fusion(f32[1,136,264]{2,1,0:T(8,128)S(1)} %get-tuple-element.181, f32[]{:T(128)} %bitcast.40, f32[]{:T(128)} %bitcast.39, f32[]{:T(128)} %bitcast.38, f32[]{:T(128)} %bitcast.37, f32[]{:T(128)} %bitcast.36, f32[]{:T(128)} %bitcast.35, f32[]{:T(128)} %bitcast.34, f32[]{:T(128)} %bitcast.33, f32[]{:T(128)} %bitcast.31), kind=kLoop, calls=%fused_computation.124 | loop fusion | flops 574464 | bytes 1351716 | tf_op jit(solution)/shard_map/add | solution.py:32
  46.1 5.9 %fusion.138 = bf16[1,1,128,256]{3,2,1,0:T(8,128)(2,1)S(1)} fusion(f32[1,128,264]{2,1,0:T(8,128)S(1)} %fusion.103, f32[]{:T(128)} %bitcast.40, f32[]{:T(128)} %bitcast.39, f32[]{:T(128)} %bitcast.38, f32[]{:T(128)} %bitcast.37, f32[]{:T(128)} %bitcast.36, f32[]{:T(128)} %bitcast.35, f32[]{:T(128)} %bitcast.34, f32[]{:T(128)} %bitcast.33, f32[]{:T(128)} %bitcast.31), kind=kLoop, calls=%fused_computation.196 | loop fusion | flops 589824 | bytes 1245220 | tf_op jit(solution)/shard_map/stack | solution.py:96
  52.7 65.6 %all-gather.2.cloned.1.call-done = bf16[32,2,128,256]{3,2,1,0:T(8,128)(2,1)} async-done(((bf16[1,2,128,256]{3,2,1,0:T(8,128)(2,1)}), bf16[32,2,128,256]{3,2,1,0:T(8,128)(2,1)}) %all-gather.2.cloned.1.call-update) | async-done | bytes 4194320 | tf_op jit(solution)/shard_map/all_gather | solution.py:97
  118.3 1.9 fusion.142
  120.2 3.1 collective-permute-start.4
  123.3 1.3 collective-permute-start.5
  124.6 20.9 %collective-permute-done.4 = bf16[32,2,32,256]{3,2,1,0:T(8,128)(2,1)S(1)} collective-permute-done((bf16[32,2,32,256]{3,2,1,0:T(8,128)(2,1)S(1)}, bf16[32,2,32,256]{3,2,1,0:T(8,128)(2,1)S(1)}, u32[]{:S(2)}, u32[]{:S(2)}) %collective-permute-start.4) | collective-permute-done | bytes 1048608 | tf_op jit(solution)/shard_map/ppermute | solution.py:18
  145.9 3.5 %collective-permute-done.5 = bf16[32,2,32,256]{3,2,1,0:T(8,128)(2,1)S(1)} collective-permute-done((bf16[32,2,32,256]{3,2,1,0:T(8,128)(2,1)S(1)}, bf16[32,2,32,256]{3,2,1,0:T(8,128)(2,1)S(1)}, u32[]{:S(2)}, u32[]{:S(2)}) %collective-permute-start.5) | collective-permute-done | bytes 1048608 | tf_op jit(solution)/shard_map/ppermute | solution.py:20
  149.5 3.7 %fusion.141 = (bf16[32,2,192,32]{3,2,1,0:T(8,128)(2,1)}, bf16[32,2,192,32]{3,2,1,0:T(8,128)(2,1)S(1)}) fusion(bf16[32,2,192,256]{3,2,1,0:T(8,128)(2,1)S(1)} %constant_dynamic-update-slice_fusion), kind=kLoop, calls=%fused_computation.205 | loop fusion | bytes 3145728 | tf_op jit(solution)/shard_map/slice | solution.py:15
  153.2 4.1 %copy.8 = bf16[32,2,192,32]{2,3,1,0:T(8,128)(2,1)} copy(bf16[32,2,192,32]{3,2,1,0:T(8,128)(2,1)} %get-tuple-element.176) | data formatting | bytes 1572864 | tf_op jit(solution)/shard_map/slice | solution.py:15
  157.3 3.1 collective-permute-start.6
  160.4 3.0 copy.9
  163.4 1.5 collective-permute-start.7
  164.9 15.9 %collective-permute-done.6 = bf16[32,2,192,32]{2,3,1,0:T(8,128)(2,1)} collective-permute-done((bf16[32,2,192,32]{2,3,1,0:T(8,128)(2,1)}, bf16[32,2,192,32]{2,3,1,0:T(8,128)(2,1)}, u32[]{:S(2)}, u32[]{:S(2)}) %collective-permute-start.6) | collective-permute-done | bytes 786464 | tf_op jit(solution)/shard_map/ppermute | solution.py:18
  180.8 3.4 %copy.10 = bf16[32,2,192,32]{3,2,1,0:T(8,128)(2,1)S(1)} copy(bf16[32,2,192,32]{2,3,1,0:T(8,128)(2,1)} %collective-permute-done.6) | data formatting | bytes 1572864 | tf_op jit(solution)/shard_map/ppermute | solution.py:18
  184.2 4.4 %collective-permute-done.7 = bf16[32,2,192,32]{2,3,1,0:T(8,128)(2,1)} collective-permute-done((bf16[32,2,192,32]{2,3,1,0:T(8,128)(2,1)}, bf16[32,2,192,32]{2,3,1,0:T(8,128)(2,1)}, u32[]{:S(2)}, u32[]{:S(2)}) %collective-permute-start.7) | collective-permute-done | bytes 786464 | tf_op jit(solution)/shard_map/ppermute | solution.py:20
  188.6 3.9 %copy.11 = bf16[32,2,192,32]{3,2,1,0:T(8,128)(2,1)} copy(bf16[32,2,192,32]{2,3,1,0:T(8,128)(2,1)} %collective-permute-done.7) | data formatting | bytes 1572864 | tf_op jit(solution)/shard_map/ppermute | solution.py:20
  192.4 11.6 %pad_maximum_fusion = bf16[32,2,192,320]{3,2,1,0:T(8,128)(2,1)} fusion(bf16[32,2,192,32]{3,2,1,0:T(8,128)(2,1)} %copy.11, bf16[32,2,192,256]{3,2,1,0:T(8,128)(2,1)} %copy-done, bf16[32,2,192,32]{3,2,1,0:T(8,128)(2,1)S(1)} %copy.10), kind=kLoop, calls=%fused_computation.117 | loop fusion | flops 23592960 | bytes 15728640 | tf_op jit(solution)/shard_map/concatenate | solution.py:16
  204.1 106.6 %while.15 = (s32[]{:T(128)}, f32[6,2,128,256]{3,2,0,1:T(8,128)}, s32[6,2]{0,1:T(2,128)S(1)}, s32[32]{0:T(128)S(1)}, bf16[32,2,192,320]{3,2,1,0:T(8,128)(2,1)}, /*index=5*/s32[]{:T(128)}) while((s32[]{:T(128)}, f32[6,2,128,256]{3,2,0,1:T(8,128)}, s32[6,2]{0,1:T(2,128)S(1)}, s32[32]{0:T(128)S(1)}, bf16[32,2,192,320]{3,2,1,0:T(8,128)(2,1)}, ...), condition=%wide.region_2.3_spmd, body=%wide.region_1.2_spmd.sunk | while | flops 2396370688 | bytes 19467128 | solution.py:84
  204.7 1.3 fusion.177
  206.0 1.3 fusion.176
  207.3 7.6 %fusion.178 = bf16[32,2,128,320]{2,3,0,1:T(8,128)(2,1)S(1)} fusion(bf16[32,2,192,320]{3,2,1,0:T(8,128)(2,1)} %get-tuple-element.288, s32[32]{0:T(128)S(1)} %get-tuple-element.267, s32[128,192]{1,0:T(8,128)S(1)} %iota_subtract_fusion.5, bf16[32]{0:T(256)(128)(2,1)S(1)} %get-tuple-element.268, ...), kind=kOutput, calls=%fused_computation.19.clone.clone.clone.clone.clone.2.clone.1 | convolution fusion | flops 1022623744 | bytes 13205888 | tf_op jit(solution)/shard_map/while/body/eval_jaxpr/erp,eipk->eirk/dot_general | solution.py:79
  215.0 6.9 %fusion.179 = f32[6,2,128,256]{3,2,0,1:T(8,128)} fusion(f32[6,2,128,256]{3,2,0,1:T(8,128)} %get-tuple-element.279, s32[]{:T(128)} %get-tuple-element.278, s32[32]{0:T(128)S(1)} %get-tuple-element.260, s32[256,320]{0,1:T(8,128)S(1)} %iota_subtract_fusion.4, bf16[32]{0:T(256)(128)(2,1)S(1)} %get-tuple-element.263, ...), kind=kOutput, calls=%fused_computation.47.clone.3 | convolution fusion | flops 1373634560 | bytes 5833600 | tf_op jit(solution)/shard_map/while/body/eval_jaxpr/eirk,eck->irc/dot_general | solution.py:82
  222.5 1.3 fusion.177
  223.8 1.3 fusion.176
  225.1 7.6 %fusion.178 = bf16[32,2,128,320]{2,3,0,1:T(8,128)(2,1)S(1)} fusion(bf16[32,2,192,320]{3,2,1,0:T(8,128)(2,1)} %get-tuple-element.288, s32[32]{0:T(128)S(1)} %get-tuple-element.267, s32[128,192]{1,0:T(8,128)S(1)} %iota_subtract_fusion.5, bf16[32]{0:T(256)(128)(2,1)S(1)} %get-tuple-element.268, ...), kind=kOutput, calls=%fused_computation.19.clone.clone.clone.clone.clone.2.clone.1 | convolution fusion | flops 1022623744 | bytes 13205888 | tf_op jit(solution)/shard_map/while/body/eval_jaxpr/erp,eipk->eirk/dot_general | solution.py:79
  232.8 6.9 %fusion.179 = f32[6,2,128,256]{3,2,0,1:T(8,128)} fusion(f32[6,2,128,256]{3,2,0,1:T(8,128)} %get-tuple-element.279, s32[]{:T(128)} %get-tuple-element.278, s32[32]{0:T(128)S(1)} %get-tuple-element.260, s32[256,320]{0,1:T(8,128)S(1)} %iota_subtract_fusion.4, bf16[32]{0:T(256)(128)(2,1)S(1)} %get-tuple-element.263, ...), kind=kOutput, calls=%fused_computation.47.clone.3 | convolution fusion | flops 1373634560 | bytes 5833600 | tf_op jit(solution)/shard_map/while/body/eval_jaxpr/eirk,eck->irc/dot_general | solution.py:82
  240.3 1.3 fusion.177
  242.9 7.6 %fusion.178 = bf16[32,2,128,320]{2,3,0,1:T(8,128)(2,1)S(1)} fusion(bf16[32,2,192,320]{3,2,1,0:T(8,128)(2,1)} %get-tuple-element.288, s32[32]{0:T(128)S(1)} %get-tuple-element.267, s32[128,192]{1,0:T(8,128)S(1)} %iota_subtract_fusion.5, bf16[32]{0:T(256)(128)(2,1)S(1)} %get-tuple-element.268, ...), kind=kOutput, calls=%fused_computation.19.clone.clone.clone.clone.clone.2.clone.1 | convolution fusion | flops 1022623744 | bytes 13205888 | tf_op jit(solution)/shard_map/while/body/eval_jaxpr/erp,eipk->eirk/dot_general | solution.py:79
  250.6 6.9 %fusion.179 = f32[6,2,128,256]{3,2,0,1:T(8,128)} fusion(f32[6,2,128,256]{3,2,0,1:T(8,128)} %get-tuple-element.279, s32[]{:T(128)} %get-tuple-element.278, s32[32]{0:T(128)S(1)} %get-tuple-element.260, s32[256,320]{0,1:T(8,128)S(1)} %iota_subtract_fusion.4, bf16[32]{0:T(256)(128)(2,1)S(1)} %get-tuple-element.263, ...), kind=kOutput, calls=%fused_computation.47.clone.3 | convolution fusion | flops 1373634560 | bytes 5833600 | tf_op jit(solution)/shard_map/while/body/eval_jaxpr/eirk,eck->irc/dot_general | solution.py:82
  258.0 1.3 fusion.177
  260.7 7.6 %fusion.178 = bf16[32,2,128,320]{2,3,0,1:T(8,128)(2,1)S(1)} fusion(bf16[32,2,192,320]{3,2,1,0:T(8,128)(2,1)} %get-tuple-element.288, s32[32]{0:T(128)S(1)} %get-tuple-element.267, s32[128,192]{1,0:T(8,128)S(1)} %iota_subtract_fusion.5, bf16[32]{0:T(256)(128)(2,1)S(1)} %get-tuple-element.268, ...), kind=kOutput, calls=%fused_computation.19.clone.clone.clone.clone.clone.2.clone.1 | convolution fusion | flops 1022623744 | bytes 13205888 | tf_op jit(solution)/shard_map/while/body/eval_jaxpr/erp,eipk->eirk/dot_general | solution.py:79
  268.3 6.9 %fusion.179 = f32[6,2,128,256]{3,2,0,1:T(8,128)} fusion(f32[6,2,128,256]{3,2,0,1:T(8,128)} %get-tuple-element.279, s32[]{:T(128)} %get-tuple-element.278, s32[32]{0:T(128)S(1)} %get-tuple-element.260, s32[256,320]{0,1:T(8,128)S(1)} %iota_subtract_fusion.4, bf16[32]{0:T(256)(128)(2,1)S(1)} %get-tuple-element.263, ...), kind=kOutput, calls=%fused_computation.47.clone.3 | convolution fusion | flops 1373634560 | bytes 5833600 | tf_op jit(solution)/shard_map/while/body/eval_jaxpr/eirk,eck->irc/dot_general | solution.py:82
  275.8 1.3 fusion.177
  278.4 7.6 %fusion.178 = bf16[32,2,128,320]{2,3,0,1:T(8,128)(2,1)S(1)} fusion(bf16[32,2,192,320]{3,2,1,0:T(8,128)(2,1)} %get-tuple-element.288, s32[32]{0:T(128)S(1)} %get-tuple-element.267, s32[128,192]{1,0:T(8,128)S(1)} %iota_subtract_fusion.5, bf16[32]{0:T(256)(128)(2,1)S(1)} %get-tuple-element.268, ...), kind=kOutput, calls=%fused_computation.19.clone.clone.clone.clone.clone.2.clone.1 | convolution fusion | flops 1022623744 | bytes 13205888 | tf_op jit(solution)/shard_map/while/body/eval_jaxpr/erp,eipk->eirk/dot_general | solution.py:79
  286.1 6.9 %fusion.179 = f32[6,2,128,256]{3,2,0,1:T(8,128)} fusion(f32[6,2,128,256]{3,2,0,1:T(8,128)} %get-tuple-element.279, s32[]{:T(128)} %get-tuple-element.278, s32[32]{0:T(128)S(1)} %get-tuple-element.260, s32[256,320]{0,1:T(8,128)S(1)} %iota_subtract_fusion.4, bf16[32]{0:T(256)(128)(2,1)S(1)} %get-tuple-element.263, ...), kind=kOutput, calls=%fused_computation.47.clone.3 | convolution fusion | flops 1373634560 | bytes 5833600 | tf_op jit(solution)/shard_map/while/body/eval_jaxpr/eirk,eck->irc/dot_general | solution.py:82
  293.6 1.3 fusion.177
  296.2 7.6 %fusion.178 = bf16[32,2,128,320]{2,3,0,1:T(8,128)(2,1)S(1)} fusion(bf16[32,2,192,320]{3,2,1,0:T(8,128)(2,1)} %get-tuple-element.288, s32[32]{0:T(128)S(1)} %get-tuple-element.267, s32[128,192]{1,0:T(8,128)S(1)} %iota_subtract_fusion.5, bf16[32]{0:T(256)(128)(2,1)S(1)} %get-tuple-element.268, ...), kind=kOutput, calls=%fused_computation.19.clone.clone.clone.clone.clone.2.clone.1 | convolution fusion | flops 1022623744 | bytes 13205888 | tf_op jit(solution)/shard_map/while/body/eval_jaxpr/erp,eipk->eirk/dot_general | solution.py:79
  303.8 6.9 %fusion.179 = f32[6,2,128,256]{3,2,0,1:T(8,128)} fusion(f32[6,2,128,256]{3,2,0,1:T(8,128)} %get-tuple-element.279, s32[]{:T(128)} %get-tuple-element.278, s32[32]{0:T(128)S(1)} %get-tuple-element.260, s32[256,320]{0,1:T(8,128)S(1)} %iota_subtract_fusion.4, bf16[32]{0:T(256)(128)(2,1)S(1)} %get-tuple-element.263, ...), kind=kOutput, calls=%fused_computation.47.clone.3 | convolution fusion | flops 1373634560 | bytes 5833600 | tf_op jit(solution)/shard_map/while/body/eval_jaxpr/eirk,eck->irc/dot_general | solution.py:82
  310.7 2.4 multiply_bitcast_fusion
  (60 shorter events, 16.7 us)
Async XLA Ops:
  6.5 111.8 %all-gather.2.cloned.1.call-start = ((), (), s32[]{:S(2)}) async-start(), calls=%async_computation | async-start | bytes 4325376 | tf_op jit(solution)/shard_map/all_gather | solution.py:97
  8.2 7.9 %collective-permute-start = (f32[2,1,4,256]{3,2,1,0:T(4,128)S(1)}, f32[2,1,4,256]{3,2,1,0:T(4,128)S(1)}, u32[]{:S(2)}, u32[]{:S(2)}) collective-permute-start(f32[2,1,4,256]{3,2,1,0:T(4,128)S(1)} %get-tuple-element.184), channel_id=1, source_target_pairs={{0,64},{64,128},{128,192},{1,65},{65,129},{129,193},{2,66},{66,130... | collective-permute-start | bytes 24584 | tf_op jit(solution)/shard_map/ppermute | solution.py:18
  12.3 4.4 %collective-permute-start.1 = (f32[2,1,4,256]{3,2,1,0:T(4,128)S(1)}, f32[2,1,4,256]{3,2,1,0:T(4,128)S(1)}, u32[]{:S(2)}, u32[]{:S(2)}) collective-permute-start(f32[2,1,4,256]{3,2,1,0:T(4,128)S(1)} %get-tuple-element.185), channel_id=1, source_target_pairs={{64,0},{128,64},{192,128},{65,1},{129,65},{193,129},{66,2},{130,66... | collective-permute-start | bytes 24584 | tf_op jit(solution)/shard_map/ppermute | solution.py:20
  17.7 5.6 %collective-permute-start.2 = (f32[2,1,136,4]{3,2,1,0:T(8,128)S(1)}, f32[2,1,136,4]{3,2,1,0:T(8,128)S(1)}, u32[]{:S(2)}, u32[]{:S(2)}) collective-permute-start(f32[2,1,136,4]{3,2,1,0:T(8,128)S(1)} %get-tuple-element.182), channel_id=1, source_target_pairs={{0,32},{1,33},{2,34},{3,35},{4,36},{5,37},{6,38},{7,39},{8,40},{9,... | collective-permute-start | bytes 13064 | tf_op jit(solution)/shard_map/ppermute | solution.py:18
  21.3 5.8 %collective-permute-start.3 = (f32[2,1,136,4]{3,2,1,0:T(8,128)S(1)}, f32[2,1,136,4]{3,2,1,0:T(8,128)S(1)}, u32[]{:S(2)}, u32[]{:S(2)}) collective-permute-start(f32[2,1,136,4]{3,2,1,0:T(8,128)S(1)} %get-tuple-element.183), channel_id=1, source_target_pairs={{32,0},{33,1},{34,2},{35,3},{36,4},{37,5},{38,6},{39,7},{40,8},{41... | collective-permute-start | bytes 13064 | tf_op jit(solution)/shard_map/ppermute | solution.py:20
  118.3 27.3 %copy-start.1 = (bf16[32,2,128,256]{3,2,1,0:T(8,128)(2,1)S(1)}, bf16[32,2,128,256]{3,2,1,0:T(8,128)(2,1)}, u32[]{:S(2)}) copy-start(bf16[32,2,128,256]{3,2,1,0:T(8,128)(2,1)} %all-gather.2.cloned.1.call-done) | copy-start | bytes 12582916
  120.2 25.3 %collective-permute-start.4 = (bf16[32,2,32,256]{3,2,1,0:T(8,128)(2,1)S(1)}, bf16[32,2,32,256]{3,2,1,0:T(8,128)(2,1)S(1)}, u32[]{:S(2)}, u32[]{:S(2)}) collective-permute-start(bf16[32,2,32,256]{3,2,1,0:T(8,128)(2,1)S(1)} %get-tuple-element.179), channel_id=1, source_target_pairs={{0,64},{64,128},{128,192},{1,65},{65,129},{129,193},{2,66},{66,130... | collective-permute-start | bytes 3145736 | tf_op jit(solution)/shard_map/ppermute | solution.py:18
  123.3 26.1 %collective-permute-start.5 = (bf16[32,2,32,256]{3,2,1,0:T(8,128)(2,1)S(1)}, bf16[32,2,32,256]{3,2,1,0:T(8,128)(2,1)S(1)}, u32[]{:S(2)}, u32[]{:S(2)}) collective-permute-start(bf16[32,2,32,256]{3,2,1,0:T(8,128)(2,1)S(1)} %get-tuple-element.178), channel_id=1, source_target_pairs={{64,0},{128,64},{192,128},{65,1},{129,65},{193,129},{66,2},{130,66... | collective-permute-start | bytes 3145736 | tf_op jit(solution)/shard_map/ppermute | solution.py:20
  149.5 3.7 %copy-start = (bf16[32,2,192,256]{3,2,1,0:T(8,128)(2,1)}, bf16[32,2,192,256]{3,2,1,0:T(8,128)(2,1)S(1)}, u32[]{:S(2)}) copy-start(bf16[32,2,192,256]{3,2,1,0:T(8,128)(2,1)S(1)} %constant_dynamic-update-slice_fusion) | copy-start | bytes 18874372
  157.3 23.5 %collective-permute-start.6 = (bf16[32,2,192,32]{2,3,1,0:T(8,128)(2,1)}, bf16[32,2,192,32]{2,3,1,0:T(8,128)(2,1)}, u32[]{:S(2)}, u32[]{:S(2)}) collective-permute-start(bf16[32,2,192,32]{2,3,1,0:T(8,128)(2,1)} %copy.8), channel_id=1, source_target_pairs={{0,32},{1,33},{2,34},{3,35},{4,36},{5,37},{6,38},{7,39},{8,40},{9,... | collective-permute-start | bytes 2359304 | tf_op jit(solution)/shard_map/ppermute | solution.py:18
  163.4 25.2 %collective-permute-start.7 = (bf16[32,2,192,32]{2,3,1,0:T(8,128)(2,1)}, bf16[32,2,192,32]{2,3,1,0:T(8,128)(2,1)}, u32[]{:S(2)}, u32[]{:S(2)}) collective-permute-start(bf16[32,2,192,32]{2,3,1,0:T(8,128)(2,1)} %copy.9), channel_id=1, source_target_pairs={{32,0},{33,1},{34,2},{35,3},{36,4},{37,5},{38,6},{39,7},{40,8},{41... | collective-permute-start | bytes 2359304 | tf_op jit(solution)/shard_map/ppermute | solution.py:20
  192.4 11.6 %copy-start.2 = (s32[32]{0:T(128)S(1)}, s32[32]{0:T(128)}, u32[]{:S(2)}) copy-start(s32[32]{0:T(128)} %param.10) | copy-start | bytes 388
  192.4 11.6 %copy-start.3 = (s32[6,2]{0,1:T(2,128)S(1)}, s32[6,2]{0,1:T(2,128)}, u32[]{:S(2)}) copy-start(s32[6,2]{0,1:T(2,128)} %param.11) | copy-start | bytes 148
Sparse Core Ops, SparseCore 0:
  52.8 65.4 all-gather.1
where the time goes:
time: 322 us; the launch traced here: 320 us
  waiting for transfers between devices  115 us (36%)
  matrix products  86.9 us (27%)
  other arithmetic  60.5 us (19%)
  local copies, waits for them, and re-layouts  25 us (8%)
  starting transfers between devices  19.1 us (6%)
  between operations  13.6 us (4%)
    all_gather x1, waiting for transfers between devices, shards(): every_epoch = lax.all_gather(images, 'ea', axis=0, tiled=True)  65.6 us
    dot_general x6, matrix products, one_hyp(): jnp.einsum('erp,eipk->eirk', row_band, padded, preferred_element_type=jnp...  45.7 us
    dot_general x6, matrix products, one_hyp(): jnp.einsum('eirk,eck->irc', moved_rows, col_band, preferred_element_type=...  41.3 us
    ppermute x4, waiting for transfers between devices, extended(): lax.ppermute(tail, axis, [(i, (i + 1) % count) for i in range(ends)])  36.8 us
    ppermute x4, starting transfers between devices, extended(): lax.ppermute(tail, axis, [(i, (i + 1) % count) for i in range(ends)])  13.7 us
    concatenate x3, other arithmetic, extended(): jnp.concatenate([lax.ppermute(tail, axis, [(i, (i + 1) % count) for i in...  13.7 us
    another operation x3, other arithmetic, shards(): images = jnp.stack([psi, phi], 1)  12.7 us
    ppermute x4, waiting for transfers between devices, extended(): lax.ppermute(head, axis, [((i + 1) % count, i) for i in range(ends)])  12.2 us
  transfers between devices with their start and end apart: 9, of which 7 were waited for; matrix products, arithmetic and copies ran while one was open for 3% of the time, Pallas kernels for 0%

commit v1 on v0

v1 whole, which is shorter than its diff:
```python
import functools

import jax
import jax.numpy as jnp
import numpy as np
from jax import lax
from jax.experimental import pallas as pl
from jax.experimental.pallas import tpu as pltpu
from jax.sharding import PartitionSpec as P

MESH = pl.DeviceIdType.MESH
F32 = jnp.float32
BF16 = jnp.bfloat16
ROWS, COLS = 128, 256
HALO = 32
EDGE = 40
TAPS = 9
SPAN = COLS + HALO
EPOCHS = 32
GROUP = 8
FRACS = 16
HALF = SPAN // 2


def spline_table():
    frac = np.arange(FRACS, dtype=np.float32) / np.float32(16.0)
    frac2 = frac * frac
    frac3 = frac2 * frac
    one = np.float32(1.0)
    table = np.stack(
        [
            (one - frac) ** 3 / 6,
            (3 * frac3 - 6 * frac2 + 4) / 6,
            (-3 * frac3 + 3 * frac2 + 3 * frac + 1) / 6,
            frac3 / 6,
        ],
        -1,
    )
    return table.astype(np.float32).astype(BF16).astype(np.float32)


def shift_of(speed, time):
    moved = lax.shift_right_arithmetic(speed * time, 3)
    return lax.shift_right_arithmetic(moved, 4), lax.bitwise_and(moved, 15)


def band(offset, weights):
    out = jnp.zeros(offset.shape, F32)
    for a in range(4):
        out = jnp.where(offset == a, weights[a], out)
    return out


def build_templates(wtab, ty, col_main, col_rim, row_tmpl):
    k = lax.broadcasted_iota(jnp.int32, (320, 128), 1)
    u = lax.broadcasted_iota(jnp.int32, (320, 128), 0)
    main_offset = k - u + 33
    k2 = lax.broadcasted_iota(jnp.int32, (320, 128), 1) % 32 + jnp.where(ty == 0, COLS, -HALO)
    u2 = lax.broadcasted_iota(jnp.int32, (320, 128), 0)
    rim_offset = k2 - u2 + 33
    v = lax.broadcasted_iota(jnp.int32, (256, 128), 0)
    r = lax.broadcasted_iota(jnp.int32, (256, 128), 1)
    row_offset = v - 64 - r + 1

    @pl.loop(0, FRACS)
    def _(f):
        weights = [wtab[f, a] for a in range(4)]
        col_main[f, 0] = band(main_offset, weights)
        col_main[f, 1] = band(main_offset + 128, weights)
        col_rim[f] = band(rim_offset, weights)
        row_tmpl[f] = band(row_offset, weights)


def move_rows(epoch, place, times, vel, hyps, images, row_tmpl, rhs, moved):
    time = times[epoch]
    for h in range(hyps):
        whole, frac = shift_of(vel[h, 0], time)
        lanes = slice(h * ROWS, (h + 1) * ROWS)
        rhs[0:128, lanes] = row_tmpl[frac, pl.ds(64 - whole, 128), :].astype(BF16)
        rhs[128:160, lanes] = row_tmpl[frac, pl.ds(32 - whole, 32), :].astype(BF16)
        rhs[160:192, lanes] = row_tmpl[frac, pl.ds(192 - whole, 32), :].astype(BF16)
    rims = images[epoch, 2]
    swapped = jnp.concatenate([rims[:, 64:], rims[:, :64]], axis=1)
    left = (
        jnp.concatenate([images[epoch, 0], rims], axis=1),
        jnp.concatenate([images[epoch, 1], swapped], axis=1),
    )
    for pair in range(hyps // 2):
        right = rhs[:, pair * 256 : (pair + 1) * 256]
        for i in range(2):
            res = jnp.dot(left[i], right, preferred_element_type=F32).astype(BF16)
            for q in range(2):
                h = 2 * pair + q
                part = res[:, q * ROWS : (q + 1) * ROWS]
                main = pl.multiple_of(place * COLS, COLS)
                rim = pl.multiple_of(GROUP * COLS + place * HALO, HALO)
                moved[h, pl.ds(main, COLS), i * ROWS : (i + 1) * ROWS] = part[:COLS]
                moved[h, pl.ds(rim, HALO), i * ROWS : (i + 1) * ROWS] = part[COLS:]


def add_columns(h, first, times, vel, col_main, col_rim, bands, moved, acc):
    shifts = [shift_of(vel[h, 1], times[first + p]) for p in range(GROUP)]
    for p in range(GROUP):
        whole, frac = shifts[p]
        for q in range(2):
            lanes = slice(p * COLS + q * 128, p * COLS + (q + 1) * 128)
            bands[:, lanes] = col_main[frac, q, pl.ds(32 + whole, COLS), :].astype(BF16)
    group_of_lane = lax.broadcasted_iota(jnp.int32, (COLS, 128), 1) // 32
    for q in range(GROUP // 4):
        tile = None
        for p in range(4):
            whole, frac = shifts[4 * q + p]
            rows = col_rim[frac, pl.ds(32 + whole, COLS), :]
            tile = rows if tile is None else jnp.where(group_of_lane == p, rows, tile)
        bands[:, GROUP * COLS + q * 128 : GROUP * COLS + (q + 1) * 128] = tile.astype(BF16)
    acc[h] += jnp.dot(bands[...], moved[h], preferred_element_type=F32)


def kernel(
    hyps,
    times,
    vel,
    wtab,
    taps,
    science,
    inv_variance,
    out,
    images,
    raw,
    turned,
    col_main,
    col_rim,
    row_tmpl,
    rhs,
    moved,
    bands,
    acc,
    edge_send,
    edge_recv,
    send_sems,
    recv_sems,
):
    tx, ty, me = lax.axis_index("tx"), lax.axis_index("ty"), lax.axis_index("ea")
    core, x, z = lax.rem(me, 2), lax.rem(lax.div(me, 2), 4), lax.div(me, 8)

    def ident(dz, dx, other=False):
        c = 1 - core if other else core
        return lax.rem(z + dz, 4) * 8 + lax.rem(x + dx, 4) * 2 + c

    up, down = {"tx": lax.rem(tx + 3, 4)}, {"tx": lax.rem(tx + 1, 4)}
    beside = {"ty": 1 - ty}
    z_up, z_down = {"ea": ident(1, 0)}, {"ea": ident(3, 0)}
    x_up, x_down = {"ea": ident(0, 1)}, {"ea": ident(0, 3)}
    twin = {"ea": ident(0, 0, True)}

    barrier = pltpu.get_barrier_semaphore()
    for peer in (up, down, beside, z_up, z_down, x_up, x_down, twin):
        pl.semaphore_signal(barrier, inc=1, device_id=peer, device_id_type=MESH)

    ivar = inv_variance[0]
    raw[0, EDGE : EDGE + ROWS] = science[0] * ivar
    raw[1, EDGE : EDGE + ROWS] = ivar
    pl.semaphore_wait(barrier, 8)

    def edge_copy(src, dst, n, peer):
        return pltpu.make_async_remote_copy(
            src_ref=src, dst_ref=dst, send_sem=edge_send.at[n], recv_sem=edge_recv.at[n], device_id=peer, device_id_type=MESH
        )

    to_up = edge_copy(raw.at[:, EDGE : 2 * EDGE], raw.at[:, EDGE + ROWS : 2 * EDGE + ROWS], 0, up)
    to_down = edge_copy(raw.at[:, ROWS : ROWS + EDGE], raw.at[:, 0:EDGE], 1, down)
    to_up.start()
    to_down.start()

    build_templates(wtab, ty, col_main, col_rim, row_tmpl)
    rhs[192:256] = jnp.zeros((64, hyps * ROWS), BF16)
    acc[...] = jnp.zeros_like(acc)

    tap_p = taps[...] / jnp.sum(taps[...], axis=1, keepdims=True)
    tap_q = tap_p * tap_p

    def tap(which, t):
        return (tap_p, tap_q)[which][0:1, t : t + 1]

    to_up.wait()
    to_down.wait()
    for i in range(2):
        raw[i, 0:EDGE] = jnp.where(tx == 0, 0.0, raw[i, 0:EDGE])
        raw[i, EDGE + ROWS :] = jnp.where(tx == 3, 0.0, raw[i, EDGE + ROWS :])

    def row_blur(i, start, size):
        total = None
        for t in range(TAPS):
            term = tap(i, t) * raw[i, start + t - 4 : start + t - 4 + size]
            total = term if total is None else total + term
        return total

    far = jnp.where(ty == 0, 0, EDGE + COLS)
    near = jnp.where(ty == 0, EDGE + COLS, 0)
    rims = []
    for i in range(2):
        turned[i, EDGE : EDGE + COLS] = row_blur(i, EDGE, ROWS).T
        rims.append(jnp.where(tx == 0, 0.0, row_blur(i, EDGE - HALO, HALO)))
        rims.append(jnp.where(tx == 3, 0.0, row_blur(i, EDGE + ROWS, HALO)))
    turned[2, EDGE : EDGE + COLS] = jnp.concatenate(rims, axis=0).T
    turned[:, pl.ds(pl.multiple_of(far, 8), EDGE), :] = jnp.zeros((3, EDGE, 128), F32)
    to_beside = edge_copy(
        turned.at[:, pl.ds(pl.multiple_of(EDGE + jnp.where(ty == 0, COLS - EDGE, 0), 8), EDGE), :],
        turned.at[:, pl.ds(pl.multiple_of(far, 8), EDGE), :],
        2,
        beside,
    )
    to_beside.start()
    to_beside.wait()

    lane = lax.broadcasted_iota(jnp.int32, (1, 128), 1)

    def col_tap(b, t):
        if b < 2:
            return tap(b, t)
        return jnp.where(lane < 64, tap(0, t), tap(1, t))

    rim_start = jnp.where(ty == 0, EDGE + COLS, EDGE - HALO)
    for b in range(3):
        total, rim = None, None
        for t in range(TAPS):
            term = col_tap(b, t) * turned[b, EDGE + t - 4 : EDGE + t - 4 + COLS]
            total = term if total is None else total + term
            term = col_tap(b, t) * turned[b, pl.ds(rim_start + t - 4, HALO), :]
            rim = term if rim is None else rim + term
        images[me, b, 0:COLS] = total.astype(BF16)
        images[me, b, COLS:SPAN] = rim.astype(BF16)

    sends = []

    def view(block, part):
        if part is None:
            return images.at[block]
        return images.at[block, :, part * HALF : (part + 1) * HALF]

    def descriptor(block, part, peer, n):
        return pltpu.make_async_remote_copy(
            src_ref=view(block, part),
            dst_ref=view(block, part),
            send_sem=send_sems.at[n],
            recv_sem=recv_sems.at[block, 0 if part is None else part],
            device_id=peer,
            device_id_type=MESH,
        )

    def send(block, part, peer):
        copy = descriptor(block, part, peer, len(sends))
        copy.start()
        sends.append(copy)

    def arrived(block, part=None):
        descriptor(block, part, twin, 0).wait_recv()

    own = ident(0, 0)
    for peer in (z_up, z_down, x_up, x_down, twin):
        send(own, None, peer)

    def x_arrivals(dz):
        below, above, across = ident(dz, 3), ident(dz, 1), ident(dz, 2)
        arrived(below)
        send(below, 0, x_up)
        send(below, None, twin)
        arrived(above)
        send(above, 1, x_down)
        send(above, None, twin)
        return across

    def x_across(across):
        arrived(across, 0)
        arrived(across, 1)
        send(across, None, twin)

    def spread(block):
        send(block, None, x_up)
        send(block, None, x_down)
        send(block, None, twin)

    across0 = x_arrivals(0)
    low, high, opposite = ident(3, 0), ident(1, 0), ident(2, 0)
    arrived(low)
    send(low, 0, z_up)
    spread(low)
    arrived(high)
    send(high, 1, z_down)
    spread(high)
    x_across(across0)
    arrived(opposite, 0)
    arrived(opposite, 1)
    spread(opposite)
    acrosses = [x_arrivals(dz) for dz in (3, 1)]
    for across in acrosses:
        x_across(across)
    x_across(x_arrivals(2))
    for dz in range(4):
        for dx in range(4):
            arrived(ident(dz, dx, True))
    for copy in sends:
        copy.wait_send()

    @pl.loop(0, EPOCHS // GROUP)
    def _(g):
        first = g * GROUP

        @pl.loop(0, GROUP)
        def _(p):
            move_rows(first + p, p, times, vel, hyps, images, row_tmpl, rhs, moved)

        @pl.loop(0, hyps)
        def _(h):
            add_columns(h, first, times, vel, col_main, col_rim, bands, moved, acc)

    @pl.loop(0, hyps)
    def _(h):
        sums = acc[h]
        out[h] = (sums[:, :ROWS] / jnp.sqrt(sums[:, ROWS:])).T


def shards(science, inv_variance, psf_taps, epoch_times, velocities):
    hyps = velocities.shape[0]
    vmem = pl.BlockSpec(memory_space=pltpu.VMEM)
    smem = pl.BlockSpec(memory_space=pltpu.SMEM)
    depth = GROUP * SPAN
    return pl.pallas_call(
        functools.partial(kernel, hyps),
        out_shape=jax.ShapeDtypeStruct((hyps, ROWS, COLS), F32),
        in_specs=[smem, smem, smem, vmem, vmem, vmem],
        out_specs=vmem,
        scratch_shapes=[
            pltpu.VMEM((EPOCHS, 3, SPAN, 128), BF16),
            pltpu.VMEM((2, ROWS + 2 * EDGE, COLS), F32),
            pltpu.VMEM((3, COLS + 2 * EDGE, 128), F32),
            pltpu.VMEM((FRACS, 2, 320, 128), F32),
            pltpu.VMEM((FRACS, 320, 128), F32),
            pltpu.VMEM((FRACS, 256, 128), F32),
            pltpu.VMEM((256, hyps * ROWS), BF16),
            pltpu.VMEM((hyps, depth, 256), BF16),
            pltpu.VMEM((COLS, depth), BF16),
            pltpu.VMEM((hyps, COLS, 256), F32),
            pltpu.SemaphoreType.DMA((3,)),
            pltpu.SemaphoreType.DMA((3,)),
            pltpu.SemaphoreType.DMA((48,)),
            pltpu.SemaphoreType.DMA((EPOCHS, 2)),
        ],
        compiler_params=pltpu.CompilerParams(collective_id=0, has_side_effects=True, vmem_limit_bytes=56 << 20),
    )(epoch_times, velocities, jnp.asarray(spline_table()), psf_taps, science, inv_variance)


def solution(mesh):
    in_specs = (P("ea", "tx", "ty"), P("ea", "tx", "ty"), P("ea", None), P(), P("ea", None))
    out_specs = P("ea", "tx", "ty")
    return jax.shard_map(shards, mesh=mesh, in_specs=in_specs, out_specs=out_specs, check_vma=False)
```

time: 322 us -> 89.8 us (0.28)
  waiting for transfers between devices: 115 us -> 0 us
  matrix products: 86.9 us -> 0 us
  Pallas kernels: 0 us -> 86.2 us
  other arithmetic: 60.5 us -> 0 us
  local copies, waits for them, and re-layouts: 25 us -> 3.45 us
  starting transfers between devices: 19.1 us -> 0 us
  between operations: 13.6 us -> 0.01 us
    dot_general x12 -> x0, matrix products: 86.9 us -> none  [the longest x6 45.7 us: one_hyp(): jnp.einsum('erp,eipk->eirk', row_band, padded, preferred_element_type=jnp...]
    pallas_call x0 -> x1, Pallas kernels: none -> 86.2 us  [shards(): pl.pallas_call(functools.partial(kernel, hyps), out_shape=jax.ShapeDtypeS...]
    all_gather x1 -> x0, waiting for transfers between devices: 65.6 us -> none  [shards(): every_epoch = lax.all_gather(images, 'ea', axis=0, tiled=True)]
    ppermute x8 -> x0, waiting for transfers between devices: 49 us -> none  [the longest x4 36.8 us: extended(): lax.ppermute(tail, axis, [(i, (i + 1) % count) for i in range(ends)])]
    ppermute x8 -> x0, starting transfers between devices: 19.1 us -> none  [the longest x4 13.7 us: extended(): lax.ppermute(tail, axis, [(i, (i + 1) % count) for i in range(ends)])]
    slice x12 -> x0, local copies, waits for them, and re-layouts: 16.8 us -> none  [the longest x3 7.89 us: extended(): lax.slice_in_dim(cells, cells.shape[dim] - width, cells.shape[dim], axis=...]
    concatenate x3 -> x0, other arithmetic: 13.7 us -> none  [extended(): jnp.concatenate([lax.ppermute(tail, axis, [(i, (i + 1) % count) for i in...]
    another operation x4 -> x0, other arithmetic: 13.7 us -> none  [the longest x3 12.7 us: shards(): images = jnp.stack([psi, phi], 1)]
  transfers between devices with their start and end apart: 9 -> 0, of which waited for: 7 -> 0; matrix products, arithmetic and copies ran while one was open for 3% -> 0% of each run, Pallas kernels for 0% -> 0%
where the time goes in v1:
time: 89.8 us; the launch traced here: 89.6 us
  Pallas kernels  86.2 us (96%)
  local copies, waits for them, and re-layouts  3.45 us (4%)
    pallas_call x1, Pallas kernels, shards(): pl.pallas_call(functools.partial(kernel, hyps), out_shape=jax.ShapeDtypeS...  86.2 us
    unnamed x2, local copies, waits for them, and re-layouts  3.45 us

profile of v1, /device:TPU:1, one launch (start us, length us, event | category | flops | bytes accessed | tf_op | source)
XLA Modules:
  0.0 89.6 jit_solution(5443596879809904738)
XLA Ops:
  0.0 1.4 %copy.7.vel = s32[6,2]{1,0:T(8,128)} copy(s32[6,2]{0,1:T(2,128)} %param.10) | data formatting | bytes 96 | tf_op args[4]
  1.4 86.2 %shard_map.64 = f32[6,128,256]{2,1,0:T(8,128)} custom-call(s32[32]{0:T(128)} %times.1, s32[6,2]{1,0:T(8,128)} %copy.7.vel, f32[16,4]{1,0:T(8,128)} %constant.2.clone.wtab, f32[1,9]{1,0:T(1,128)} %taps.1, f32[1,128,256]{2,1,0:T(8,128)} %science.1, f32[1,128,256]{2,1,0:T(8,128)} %inv_variance.1), custom_call_target="tpu_custom_call" | custom-call | tf_op jit(solution)/shard_map/pallas_call | solution.py:328
  87.5 2.1 %copy.9 = f32[6,128,256]{2,1,0:T(8,128)} copy(f32[6,128,256]{2,1,0:T(8,128)} %shard_map.64) | data formatting | bytes 1572864

commit v2 on v1

--- a/solution.py
+++ b/solution.py
@@ -98,13 +98,13 @@
                 moved[h, pl.ds(rim, HALO), i * ROWS : (i + 1) * ROWS] = part[COLS:]
 
 
-def add_columns(h, first, times, vel, col_main, col_rim, bands, moved, acc):
+def add_columns(h, first, times, vel, col_main, col_rim, moved, acc):
     shifts = [shift_of(vel[h, 1], times[first + p]) for p in range(GROUP)]
+    tiles = []
     for p in range(GROUP):
         whole, frac = shifts[p]
         for q in range(2):
-            lanes = slice(p * COLS + q * 128, p * COLS + (q + 1) * 128)
-            bands[:, lanes] = col_main[frac, q, pl.ds(32 + whole, COLS), :].astype(BF16)
+            tiles.append(col_main[frac, q, pl.ds(32 + whole, COLS), :].astype(BF16))
     group_of_lane = lax.broadcasted_iota(jnp.int32, (COLS, 128), 1) // 32
     for q in range(GROUP // 4):
         tile = None
@@ -112,8 +112,8 @@
             whole, frac = shifts[4 * q + p]
             rows = col_rim[frac, pl.ds(32 + whole, COLS), :]
             tile = rows if tile is None else jnp.where(group_of_lane == p, rows, tile)
-        bands[:, GROUP * COLS + q * 128 : GROUP * COLS + (q + 1) * 128] = tile.astype(BF16)
-    acc[h] += jnp.dot(bands[...], moved[h], preferred_element_type=F32)
+        tiles.append(tile.astype(BF16))
+    acc[h] += jnp.dot(jnp.concatenate(tiles, axis=1), moved[h], preferred_element_type=F32)
 
 
 def kernel(
@@ -133,7 +133,6 @@
     row_tmpl,
     rhs,
     moved,
-    bands,
     acc,
     edge_send,
     edge_recv,
@@ -173,7 +172,7 @@
     to_down.start()
 
     build_templates(wtab, ty, col_main, col_rim, row_tmpl)
-    rhs[192:256] = jnp.zeros((64, hyps * ROWS), BF16)
+    rhs[:, 192:256] = jnp.zeros((2, 64, hyps * ROWS), BF16)
     acc[...] = jnp.zeros_like(acc)
 
     tap_p = taps[...] / jnp.sum(taps[...], axis=1, keepdims=True)
@@ -249,9 +248,8 @@
         )
 
     def send(block, part, peer):
-        copy = descriptor(block, part, peer, len(sends))
-        copy.start()
-        sends.append(copy)
+        descriptor(block, part, peer, len(sends)).start()
+        sends.append((block, part, peer))
 
     def arrived(block, part=None):
         descriptor(block, part, twin, 0).wait_recv()
@@ -260,59 +258,105 @@
     for peer in (z_up, z_down, x_up, x_down, twin):
         send(own, None, peer)
 
-    def x_arrivals(dz):
-        below, above, across = ident(dz, 3), ident(dz, 1), ident(dz, 2)
+    ids = {(dz, dx): ident(dz, dx) for dz in range(4) for dx in range(4)}
+
+    def x_arrivals(dz, forward):
+        below, above = ids[dz, 3], ids[dz, 1]
         arrived(below)
-        send(below, 0, x_up)
+        if forward:
+            send(below, 0, x_up)
         send(below, None, twin)
         arrived(above)
-        send(above, 1, x_down)
+        if forward:
+            send(above, 1, x_down)
         send(above, None, twin)
-        return across
-
-    def x_across(across):
-        arrived(across, 0)
-        arrived(across, 1)
+
+    def spread(block):
+        for peer in (x_up, x_down, twin):
+            send(block, None, peer)
+
+    def halves_arrived(block):
+        arrived(block, 0)
+        arrived(block, 1)
+
+    def start_rows():
+        x_arrivals(0, True)
+
+    def own_across():
+        across = ids[0, 2]
+        halves_arrived(across)
+        for peer in (twin, z_up, z_down):
+            send(across, None, peer)
+
+    def z_neighbours():
+        low, high = ids[3, 0], ids[1, 0]
+        arrived(low)
+        send(low, 0, z_up)
+        spread(low)
+        arrived(high)
+        send(high, 1, z_down)
+        spread(high)
+
+    def z_opposite():
+        opposite = ids[2, 0]
+        halves_arrived(opposite)
+        spread(opposite)
+
+    def z_across(dz):
+        across = ids[dz, 2]
+        arrived(across)
         send(across, None, twin)
 
-    def spread(block):
-        send(block, None, x_up)
-        send(block, None, x_down)
-        send(block, None, twin)
-
-    across0 = x_arrivals(0)
-    low, high, opposite = ident(3, 0), ident(1, 0), ident(2, 0)
-    arrived(low)
-    send(low, 0, z_up)
-    spread(low)
-    arrived(high)
-    send(high, 1, z_down)
-    spread(high)
-    x_across(across0)
-    arrived(opposite, 0)
-    arrived(opposite, 1)
-    spread(opposite)
-    acrosses = [x_arrivals(dz) for dz in (3, 1)]
-    for across in acrosses:
-        x_across(across)
-    x_across(x_arrivals(2))
-    for dz in range(4):
-        for dx in range(4):
-            arrived(ident(dz, dx, True))
-    for copy in sends:
-        copy.wait_send()
+    def last_across():
+        across = ids[2, 2]
+        halves_arrived(across)
+        send(across, None, twin)
+
+    duties = {
+        (0, 1): [start_rows],
+        (0, 3): [own_across],
+        (0, 4): [z_neighbours],
+        (0, 6): [z_opposite],
+        (1, 1): [lambda: x_arrivals(3, False)],
+        (1, 3): [lambda: z_across(3)],
+        (1, 4): [lambda: x_arrivals(1, False)],
+        (1, 6): [lambda: z_across(1)],
+        (2, 2): [lambda: x_arrivals(2, True)],
+        (2, 5): [last_across],
+    }
+    steps = 7
+
+    def attend(g, step, only):
+        for (group, at), acts in duties.items():
+            if at in only:
+
+                @pl.when(jnp.logical_and(g == group, step == at))
+                def _(acts=acts):
+                    for act in acts:
+                        act()
 
     @pl.loop(0, EPOCHS // GROUP)
     def _(g):
-        first = g * GROUP
-
-        @pl.loop(0, GROUP)
-        def _(p):
-            move_rows(first + p, p, times, vel, hyps, images, row_tmpl, rhs, moved)
-
-        @pl.loop(0, hyps)
-        def _(h):
-            add_columns(h, first, times, vel, col_main, col_rim, bands, moved, acc)
+        dz = jnp.where(g == 0, 0, jnp.where(g == 1, 3, jnp.where(g == 2, 1, 2)))
+        first = lax.rem(z + dz, 4) * GROUP
+
+        @pl.loop(0, 4)
+        def _(j):
+            attend(g, j, range(4))
+            dx = jnp.where(j == 0, 0, jnp.where(j == 1, 3, jnp.where(j == 2, 1, 2)))
+            mine, other = ident(dz, dx), ident(dz, dx, True)
+            arrived(other)
+            for n, block in enumerate((mine, other)):
+                move_rows(block, lax.rem(block, GROUP), times, vel, hyps, images, row_tmpl, rhs.at[n], moved)
+
+        @pl.loop(0, hyps // 2)
+        def _(pair):
+            attend(g, pair + 4, range(4, steps))
+            for n in range(2):
+                add_columns(2 * pair + n, first, times, vel, col_main, col_rim, moved, acc)
+
+    for n, (block, part, peer) in enumerate(sends):
+        descriptor(block, part, peer, n).wait_send()
 
     @pl.loop(0, hyps)
     def _(h):
@@ -337,9 +381,8 @@
             pltpu.VMEM((FRACS, 2, 320, 128), F32),
             pltpu.VMEM((FRACS, 320, 128), F32),
             pltpu.VMEM((FRACS, 256, 128), F32),
-            pltpu.VMEM((256, hyps * ROWS), BF16),
+            pltpu.VMEM((2, 256, hyps * ROWS), BF16),
             pltpu.VMEM((hyps, depth, 256), BF16),
-            pltpu.VMEM((COLS, depth), BF16),
             pltpu.VMEM((hyps, COLS, 256), F32),
             pltpu.SemaphoreType.DMA((3,)),
             pltpu.SemaphoreType.DMA((3,)),

time: 89.8 us -> 74.8 us (0.83)
  Pallas kernels: 86.2 us -> 71.2 us
    pallas_call x1, Pallas kernels: 86.2 us -> 71.2 us  [shards(): pl.pallas_call(functools.partial(kernel, hyps), out_shape=jax.ShapeDtypeS...]
where the time goes in v2:
time: 74.8 us; the launch traced here: 74.7 us
  Pallas kernels  71.2 us (95%)
  local copies, waits for them, and re-layouts  3.45 us (5%)
    pallas_call x1, Pallas kernels, shards(): pl.pallas_call(functools.partial(kernel, hyps), out_shape=jax.ShapeDtypeS...  71.2 us
    unnamed x2, local copies, waits for them, and re-layouts  3.45 us

profile of v2, /device:TPU:1, one launch (start us, length us, event | category | flops | bytes accessed | tf_op | source)
XLA Modules:
  0.0 74.7 jit_solution(12027720170427993423)
XLA Ops:
  0.0 1.4 %copy.7.vel = s32[6,2]{1,0:T(8,128)} copy(s32[6,2]{0,1:T(2,128)} %param.10) | data formatting | bytes 96 | tf_op args[4]
  1.4 71.2 %shard_map.64 = f32[6,128,256]{2,1,0:T(8,128)} custom-call(s32[32]{0:T(128)} %times.1, s32[6,2]{1,0:T(8,128)} %copy.7.vel, f32[16,4]{1,0:T(8,128)} %constant.2.clone.wtab, f32[1,9]{1,0:T(1,128)} %taps.1, f32[1,128,256]{2,1,0:T(8,128)} %science.1, f32[1,128,256]{2,1,0:T(8,128)} %inv_variance.1), custom_call_target="tpu_custom_call" | custom-call | tf_op jit(solution)/shard_map/pallas_call | solution.py:372
  72.6 2.1 %copy.9 = f32[6,128,256]{2,1,0:T(8,128)} copy(f32[6,128,256]{2,1,0:T(8,128)} %shard_map.64) | data formatting | bytes 1572864

commit v3 on v2

--- a/solution.py
+++ b/solution.py
@@ -71,19 +71,23 @@
         row_tmpl[f] = band(row_offset, weights)
 
 
-def move_rows(epoch, place, times, vel, hyps, images, row_tmpl, rhs, moved):
-    time = times[epoch]
+def move_rows(epoch, time, place, ty, vel, hyps, images, row_tmpl, rhs, moved):
     for h in range(hyps):
-        whole, frac = shift_of(vel[h, 0], time)
+        whole, frac = shift_of(vel[0, h], time)
         lanes = slice(h * ROWS, (h + 1) * ROWS)
         rhs[0:128, lanes] = row_tmpl[frac, pl.ds(64 - whole, 128), :].astype(BF16)
         rhs[128:160, lanes] = row_tmpl[frac, pl.ds(32 - whole, 32), :].astype(BF16)
         rhs[160:192, lanes] = row_tmpl[frac, pl.ds(192 - whole, 32), :].astype(BF16)
-    rims = images[epoch, 2]
-    swapped = jnp.concatenate([rims[:, 64:], rims[:, :64]], axis=1)
+    main_at = pl.multiple_of(jnp.where(ty == 0, 0, HALO), HALO)
+    rim_at = pl.multiple_of(jnp.where(ty == 0, COLS, 0), HALO)
+    planes = [
+        jnp.concatenate([images[epoch, b, pl.ds(main_at, COLS), :], images[epoch, b, pl.ds(rim_at, HALO), :]], axis=0)
+        for b in range(3)
+    ]
+    swapped = jnp.concatenate([planes[2][:, 64:], planes[2][:, :64]], axis=1)
     left = (
-        jnp.concatenate([images[epoch, 0], rims], axis=1),
-        jnp.concatenate([images[epoch, 1], swapped], axis=1),
+        jnp.concatenate([planes[0], planes[2]], axis=1),
+        jnp.concatenate([planes[1], swapped], axis=1),
     )
     for pair in range(hyps // 2):
         right = rhs[:, pair * 256 : (pair + 1) * 256]
@@ -99,7 +103,7 @@
 
 
 def add_columns(h, first, times, vel, col_main, col_rim, moved, acc):
-    shifts = [shift_of(vel[h, 1], times[first + p]) for p in range(GROUP)]
+    shifts = [shift_of(vel[1, h], times[first + p]) for p in range(GROUP)]
     tiles = []
     for p in range(GROUP):
         whole, frac = shifts[p]
@@ -134,6 +138,7 @@
     rhs,
     moved,
     acc,
+    when,
     edge_send,
     edge_recv,
     send_sems,
@@ -142,15 +147,14 @@
     tx, ty, me = lax.axis_index("tx"), lax.axis_index("ty"), lax.axis_index("ea")
     core, x, z = lax.rem(me, 2), lax.rem(lax.div(me, 2), 4), lax.div(me, 8)
 
-    def ident(dz, dx, other=False):
-        c = 1 - core if other else core
-        return lax.rem(z + dz, 4) * 8 + lax.rem(x + dx, 4) * 2 + c
+    def ident(dz, dx, other=0):
+        return lax.rem(z + dz, 4) * 8 + lax.rem(x + dx, 4) * 2 + lax.rem(core + other, 2)
 
     up, down = {"tx": lax.rem(tx + 3, 4)}, {"tx": lax.rem(tx + 1, 4)}
     beside = {"ty": 1 - ty}
     z_up, z_down = {"ea": ident(1, 0)}, {"ea": ident(3, 0)}
     x_up, x_down = {"ea": ident(0, 1)}, {"ea": ident(0, 3)}
-    twin = {"ea": ident(0, 0, True)}
+    twin = {"ea": ident(0, 0, 1)}
 
     barrier = pltpu.get_barrier_semaphore()
     for peer in (up, down, beside, z_up, z_down, x_up, x_down, twin):
@@ -210,7 +214,6 @@
         beside,
     )
     to_beside.start()
-    to_beside.wait()
 
     lane = lax.broadcasted_iota(jnp.int32, (1, 128), 1)
 
@@ -219,110 +222,120 @@
             return tap(b, t)
         return jnp.where(lane < 64, tap(0, t), tap(1, t))
 
-    rim_start = jnp.where(ty == 0, EDGE + COLS, EDGE - HALO)
-    for b in range(3):
-        total, rim = None, None
-        for t in range(TAPS):
-            term = col_tap(b, t) * turned[b, EDGE + t - 4 : EDGE + t - 4 + COLS]
-            total = term if total is None else total + term
-            term = col_tap(b, t) * turned[b, pl.ds(rim_start + t - 4, HALO), :]
-            rim = term if rim is None else rim + term
-        images[me, b, 0:COLS] = total.astype(BF16)
-        images[me, b, COLS:SPAN] = rim.astype(BF16)
+    base = jnp.where(ty == 0, EDGE, EDGE - HALO)
+    part_at = [pl.multiple_of(HALF * (ty if part == 0 else 1 - ty), 16) for part in range(2)]
+
+    def col_blur(part):
+        for b in range(3):
+            total = None
+            for t in range(TAPS):
+                term = col_tap(b, t) * turned[b, pl.ds(base + part_at[part] + t - 4, HALF), :]
+                total = term if total is None else total + term
+            images[me, b, pl.ds(part_at[part], HALF), :] = total.astype(BF16)
 
     sends = []
-
-    def view(block, part):
-        if part is None:
-            return images.at[block]
-        return images.at[block, :, part * HALF : (part + 1) * HALF]
+    ids = {(dz, dx): ident(dz, dx) for dz in range(4) for dx in range(4)}
+    below, above, own = ids[0, 3], ids[0, 1], ids[0, 0]
+    low, high, opposite = ids[3, 0], ids[1, 0], ids[2, 0]
 
     def descriptor(block, part, peer, n):
+        view = images.at[block] if part is None else images.at[block, :, pl.ds(part_at[part], HALF)]
         return pltpu.make_async_remote_copy(
-            src_ref=view(block, part),
-            dst_ref=view(block, part),
+            src_ref=view,
+            dst_ref=view,
             send_sem=send_sems.at[n],
             recv_sem=recv_sems.at[block, 0 if part is None else part],
             device_id=peer,
             device_id_type=MESH,
         )
 
-    def send(block, part, peer):
-        descriptor(block, part, peer, len(sends)).start()
-        sends.append((block, part, peer))
+    def send(block, part, *peers):
+        for peer in peers:
+            descriptor(block, part, peer, len(sends)).start()
+            sends.append((block, part, peer))
 
     def arrived(block, part=None):
         descriptor(block, part, twin, 0).wait_recv()
 
-    own = ident(0, 0)
-    for peer in (z_up, z_down, x_up, x_down, twin):
-        send(own, None, peer)
-
-    ids = {(dz, dx): ident(dz, dx) for dz in range(4) for dx in range(4)}
-
-    def x_arrivals(dz, forward):
-        below, above = ids[dz, 3], ids[dz, 1]
-        arrived(below)
-        if forward:
-            send(below, 0, x_up)
+    col_blur(0)
+    send(own, 0, z_up, z_down, x_up, x_down)
+    to_beside.wait()
+    col_blur(1)
+    send(own, 1, z_down, z_up, x_down, x_up)
+    send(own, None, twin)
+
+    def first_x():
+        arrived(below, 0)
+        send(below, 0, x_up)
+        arrived(above, 0)
+
+    def second_x():
+        arrived(above, 1)
+        send(above, 1, x_down)
+        arrived(below, 1)
         send(below, None, twin)
-        arrived(above)
-        if forward:
-            send(above, 1, x_down)
         send(above, None, twin)
 
-    def spread(block):
-        for peer in (x_up, x_down, twin):
-            send(block, None, peer)
-
-    def halves_arrived(block):
-        arrived(block, 0)
-        arrived(block, 1)
-
-    def start_rows():
-        x_arrivals(0, True)
+    def first_z():
+        arrived(low, 0)
+        send(low, 0, z_up, x_up, x_down)
+        arrived(high, 0)
+        send(high, 0, x_up, x_down)
 
     def own_across():
         across = ids[0, 2]
-        halves_arrived(across)
-        for peer in (twin, z_up, z_down):
-            send(across, None, peer)
-
-    def z_neighbours():
-        low, high = ids[3, 0], ids[1, 0]
-        arrived(low)
-        send(low, 0, z_up)
-        spread(low)
-        arrived(high)
-        send(high, 1, z_down)
-        spread(high)
+        arrived(across, 0)
+        arrived(across, 1)
+        send(across, None, twin)
+
+    def second_z():
+        arrived(high, 1)
+        send(high, 1, z_down, x_up, x_down)
+        arrived(low, 1)
+        send(low, 1, x_up, x_down)
+        send(low, None, twin)
+        send(high, None, twin)
 
     def z_opposite():
-        opposite = ids[2, 0]
-        halves_arrived(opposite)
-        spread(opposite)
-
-    def z_across(dz):
-        across = ids[dz, 2]
-        arrived(across)
-        send(across, None, twin)
-
-    def last_across():
-        across = ids[2, 2]
-        halves_arrived(across)
-        send(across, None, twin)
+        for part in range(2):
+            arrived(opposite, part)
+            send(opposite, part, x_up, x_down)
+        for part in range(2):
+            send(ids[0, 2], part, z_up, z_down)
+        send(opposite, None, twin)
+
+    def x_arrivals(dz):
+        for dx in (3, 1):
+            arrived(ids[dz, dx], 0)
+            arrived(ids[dz, dx], 1)
+            send(ids[dz, dx], None, twin)
+
+    def across_arrives(dz):
+        arrived(ids[dz, 2], 0)
+        arrived(ids[dz, 2], 1)
+        send(ids[dz, 2], None, twin)
+
+    def last_x(part):
+        arrived(ids[2, 3], part)
+        arrived(ids[2, 1], part)
+        if part == 0:
+            send(ids[2, 3], 0, x_up)
+        else:
+            send(ids[2, 1], 1, x_down)
+            send(ids[2, 3], None, twin)
+            send(ids[2, 1], None, twin)
 
     duties = {
-        (0, 1): [start_rows],
+        (0, 1): [first_x, first_z, second_x],
         (0, 3): [own_across],
-        (0, 4): [z_neighbours],
-        (0, 6): [z_opposite],
-        (1, 1): [lambda: x_arrivals(3, False)],
-        (1, 3): [lambda: z_across(3)],
-        (1, 4): [lambda: x_arrivals(1, False)],
-        (1, 6): [lambda: z_across(1)],
-        (2, 2): [lambda: x_arrivals(2, True)],
-        (2, 5): [last_across],
+        (0, 4): [second_z],
+        (1, 0): [z_opposite],
+        (1, 2): [lambda: x_arrivals(3)],
+        (1, 4): [lambda: x_arrivals(1)],
+        (1, 5): [lambda: last_x(0)],
+        (2, 1): [lambda: last_x(1)],
+        (2, 4): [lambda: across_arrives(3), lambda: across_arrives(1)],
+        (2, 6): [lambda: across_arrives(2)],
     }
     steps = 7
 
@@ -335,25 +348,59 @@
                     for act in acts:
                         act()
 
+    def pick(index, values):
+        out = values[-1]
+        for n in range(len(values) - 2, -1, -1):
+            out = jnp.where(index == n, values[n], out)
+        return out
+
+    order = [
+        ((0, 0, 0), (0, 0, 1)),
+        ((0, 3, 0), (0, 1, 0)),
+        ((0, 3, 1), (0, 1, 1)),
+        ((0, 2, 0), (0, 2, 1)),
+        ((3, 0, 0), (1, 0, 0)),
+        ((3, 0, 1), (1, 0, 1)),
+        ((3, 3, 0), (3, 1, 0)),
+        ((3, 3, 1), (3, 1, 1)),
+        ((1, 3, 0), (1, 1, 0)),
+        ((1, 3, 1), (1, 1, 1)),
+        ((2, 0, 0), (2, 0, 1)),
+        ((2, 3, 0), (2, 1, 0)),
+        ((2, 3, 1), (2, 1, 1)),
+        ((3, 2, 0), (1, 2, 0)),
+        ((3, 2, 1), (1, 2, 1)),
+        ((2, 2, 0), (2, 2, 1)),
+    ]
+    for n, pair in enumerate(order):
+        for m, spot in enumerate(pair):
+            when[2 * n + m] = times[ident(*spot)]
+
     @pl.loop(0, EPOCHS // GROUP)
     def _(g):
-        dz = jnp.where(g == 0, 0, jnp.where(g == 1, 3, jnp.where(g == 2, 1, 2)))
-        first = lax.rem(z + dz, 4) * GROUP
-
         @pl.loop(0, 4)
         def _(j):
             attend(g, j, range(4))
-            dx = jnp.where(j == 0, 0, jnp.where(j == 1, 3, jnp.where(j == 2, 1, 2)))
-            mine, other = ident(dz, dx), ident(dz, dx, True)
-            arrived(other)
-            for n, block in enumerate((mine, other)):
-                move_rows(block, lax.rem(block, GROUP), times, vel, hyps, images, row_tmpl, rhs.at[n], moved)
+            step = 4 * g + j
+            blocks = []
+            for m in range(2):
+                dz, dx, other = [pick(step, [pair[m][axis] for pair in order]) for axis in range(3)]
+                blocks.append(ident(dz, dx, other))
+
+                @pl.when(other == 1)
+                def _():
+                    arrived(blocks[m])
+
+            for m, block in enumerate(blocks):
+                move_rows(
+                    block, when[2 * step + m], 2 * j + m, ty, vel, hyps, images, row_tmpl, rhs.at[m], moved
+                )
 
         @pl.loop(0, hyps // 2)
         def _(pair):
             attend(g, pair + 4, range(4, steps))
             for n in range(2):
-                add_columns(2 * pair + n, first, times, vel, col_main, col_rim, moved, acc)
+                add_columns(2 * pair + n, g * GROUP, when, vel, col_main, col_rim, moved, acc)
 
     for n, (block, part, peer) in enumerate(sends):
         descriptor(block, part, peer, n).wait_send()
@@ -384,13 +431,14 @@
             pltpu.VMEM((2, 256, hyps * ROWS), BF16),
             pltpu.VMEM((hyps, depth, 256), BF16),
             pltpu.VMEM((hyps, COLS, 256), F32),
+            pltpu.SMEM((EPOCHS,), jnp.int32),
             pltpu.SemaphoreType.DMA((3,)),
             pltpu.SemaphoreType.DMA((3,)),
-            pltpu.SemaphoreType.DMA((48,)),
+            pltpu.SemaphoreType.DMA((64,)),
             pltpu.SemaphoreType.DMA((EPOCHS, 2)),
         ],
         compiler_params=pltpu.CompilerParams(collective_id=0, has_side_effects=True, vmem_limit_bytes=56 << 20),
-    )(epoch_times, velocities, jnp.asarray(spline_table()), psf_taps, science, inv_variance)
+    )(epoch_times, velocities.T, jnp.asarray(spline_table()), psf_taps, science, inv_variance)
 
 
 def solution(mesh):

time: 74.8 us -> 66.6 us (0.89)
  Pallas kernels: 71.2 us -> 64.4 us
  local copies, waits for them, and re-layouts: 3.45 us -> 2.1 us
    pallas_call x1, Pallas kernels: 71.2 us -> 64.4 us  [shards(): pl.pallas_call(functools.partial(kernel, hyps), out_shape=jax.ShapeDtypeS...]
    unnamed x2 -> x1, local copies, waits for them, and re-layouts: 3.45 us -> 2.1 us
where the time goes in v3:
time: 66.6 us; the launch traced here: 66.5 us
  Pallas kernels  64.4 us (97%)
  local copies, waits for them, and re-layouts  2.1 us (3%)
    pallas_call x1, Pallas kernels, shards(): pl.pallas_call(functools.partial(kernel, hyps), out_shape=jax.ShapeDtypeS...  64.4 us
    unnamed x1, local copies, waits for them, and re-layouts  2.1 us

profile of v3, /device:TPU:1, one launch (start us, length us, event | category | flops | bytes accessed | tf_op | source)
XLA Modules:
  0.0 66.5 jit_solution(17490434296806376822)
XLA Ops:
  0.0 64.4 %shard_map.64 = f32[6,128,256]{2,1,0:T(8,128)} custom-call(s32[32]{0:T(128)} %times.1, s32[2,6]{1,0:T(2,128)} %bitcast.1, f32[16,4]{1,0:T(8,128)} %constant.2.clone.wtab, f32[1,9]{1,0:T(1,128)} %taps.1, f32[1,128,256]{2,1,0:T(8,128)} %science.1, f32[1,128,256]{2,1,0:T(8,128)} %inv_variance.1), custom_call_target="tpu_custom_call" | custom-call | tf_op jit(solution)/shard_map/pallas_call | solution.py:419
  64.4 2.1 %copy.8 = f32[6,128,256]{2,1,0:T(8,128)} copy(f32[6,128,256]{2,1,0:T(8,128)} %shard_map.64) | data formatting | bytes 1572864

commit v4 on v3

--- a/solution.py
+++ b/solution.py
@@ -296,13 +296,13 @@
         send(low, None, twin)
         send(high, None, twin)
 
-    def z_opposite():
-        for part in range(2):
-            arrived(opposite, part)
-            send(opposite, part, x_up, x_down)
-        for part in range(2):
-            send(ids[0, 2], part, z_up, z_down)
-        send(opposite, None, twin)
+    def z_opposite(part):
+        arrived(opposite, part)
+        send(opposite, part, x_up, x_down)
+        if part == 1:
+            send(ids[0, 2], 0, z_up, z_down)
+            send(ids[0, 2], 1, z_up, z_down)
+            send(opposite, None, twin)
 
     def x_arrivals(dz):
         for dx in (3, 1):
@@ -327,12 +327,13 @@
 
     duties = {
         (0, 1): [first_x, first_z, second_x],
-        (0, 3): [own_across],
-        (0, 4): [second_z],
-        (1, 0): [z_opposite],
+        (0, 3): [second_z],
+        (0, 4): [own_across],
+        (0, 5): [lambda: z_opposite(0)],
+        (1, 0): [lambda: z_opposite(1)],
         (1, 2): [lambda: x_arrivals(3)],
-        (1, 4): [lambda: x_arrivals(1)],
-        (1, 5): [lambda: last_x(0)],
+        (1, 3): [lambda: x_arrivals(1)],
+        (1, 6): [lambda: last_x(0)],
         (2, 1): [lambda: last_x(1)],
         (2, 4): [lambda: across_arrives(3), lambda: across_arrives(1)],
         (2, 6): [lambda: across_arrives(2)],
@@ -358,12 +359,12 @@
         ((0, 0, 0), (0, 0, 1)),
         ((0, 3, 0), (0, 1, 0)),
         ((0, 3, 1), (0, 1, 1)),
-        ((0, 2, 0), (0, 2, 1)),
         ((3, 0, 0), (1, 0, 0)),
         ((3, 0, 1), (1, 0, 1)),
+        ((0, 2, 0), (0, 2, 1)),
         ((3, 3, 0), (3, 1, 0)),
+        ((1, 3, 0), (1, 1, 0)),
         ((3, 3, 1), (3, 1, 1)),
-        ((1, 3, 0), (1, 1, 0)),
         ((1, 3, 1), (1, 1, 1)),
         ((2, 0, 0), (2, 0, 1)),
         ((2, 3, 0), (2, 1, 0)),

time: 66.6 us -> 62.8 us (0.943)
  Pallas kernels: 64.4 us -> 60.5 us
    pallas_call x1, Pallas kernels: 64.4 us -> 60.5 us  [shards(): pl.pallas_call(functools.partial(kernel, hyps), out_shape=jax.ShapeDtypeS...]
where the time goes in v4:
time: 62.8 us; the launch traced here: 62.6 us
  Pallas kernels  60.5 us (96%)
  local copies, waits for them, and re-layouts  2.1 us (3%)
    pallas_call x1, Pallas kernels, shards(): pl.pallas_call(functools.partial(kernel, hyps), out_shape=jax.ShapeDtypeS...  60.5 us
    unnamed x1, local copies, waits for them, and re-layouts  2.1 us

profile of v4, /device:TPU:1, one launch (start us, length us, event | category | flops | bytes accessed | tf_op | source)
XLA Modules:
  0.0 62.6 jit_solution(14458709206270640721)
XLA Ops:
  0.0 60.5 %shard_map.64 = f32[6,128,256]{2,1,0:T(8,128)} custom-call(s32[32]{0:T(128)} %times.1, s32[2,6]{1,0:T(2,128)} %bitcast.1, f32[16,4]{1,0:T(8,128)} %constant.2.clone.wtab, f32[1,9]{1,0:T(1,128)} %taps.1, f32[1,128,256]{2,1,0:T(8,128)} %science.1, f32[1,128,256]{2,1,0:T(8,128)} %inv_variance.1), custom_call_target="tpu_custom_call" | custom-call | tf_op jit(solution)/shard_map/pallas_call | solution.py:420
  60.5 2.1 %copy.8 = f32[6,128,256]{2,1,0:T(8,128)} copy(f32[6,128,256]{2,1,0:T(8,128)} %shard_map.64) | data formatting | bytes 1572864
